TPU v7x, 32 devices: a whole 2x2x4 slice. The times are simulated.
32 devices in a mesh: lat: 4 (over y, core), lon: 8 (over z, x).
Axes of the slice: x: 2, y: 2, z: 4, core: 2. Of those that a mesh axis runs over, the one named last changes fastest.
Arguments:
- field_in: bfloat16 [512, 64, 300], P('lat', 'lon'), may hold values from -6 to 6
- sea_mask: int32 [512, 64], P('lat', 'lon'), may hold values 0 or 1
- mirror: int32 [64], replicated, may hold values from 0 to 63, as said below
- kernel: float32 [49, 300], replicated, may hold values from -0.875 to 0.875
- norm_gain: float32 [300], replicated, may hold values from 0.1 to 1.9
- proj_in: bfloat16 [300, 1200], replicated, may hold values from -0.375 to 0.375
- proj_out: bfloat16 [1200, 300], replicated, may hold values from -0.1875 to 0.1875
- cotangent: bfloat16 [512, 64, 300], P('lat', 'lon'), may hold values from -6 to 6
Outputs:
- block_out: bfloat16 [512, 64, 300], P('lat', 'lon')
- grad_field: bfloat16 [512, 64, 300], P('lat', 'lon')
- grad_in: float32 [300, 1200], replicated
- grad_out: float32 [1200, 300], replicated
- grad_kernel: float32 [49, 300], replicated
- grad_gain: float32 [300], replicated
Inputs may be any that keep to these rules, and one draw needn't show every extreme that they name: mirror[i] = (s - 1 - i) mod 64 for one s, so mirror[mirror[i]] = i.
All inputs are finite; a program needn't handle non-finite values. No bound on the sum of `sea_mask` on one device may be relied on, other than what follows from the above.
Results may differ from a plain program's by a relative error of at most 0.0057.
Values may be sent and summed in bfloat16 or wider, within the bound.
No kernel may reach another device: no remote copies, remote signals or barrier semaphores. Data moves between devices by JAX's collectives and lax.ppermute only.
A program may use at most 128 MiB of HBM per device.

v0:
```python
import jax
import jax.numpy as jnp
from jax import lax
from jax.sharding import PartitionSpec as P


def extended(block, sides, width):
    for axis, dim in sides:
        count = lax.axis_size(axis)
        forward = [(i, i + 1) for i in range(count - 1)]
        forward.append((count - 1, 0))
        backward = [(target, source) for source, target in forward]
        low = lax.ppermute(
            lax.slice_in_dim(block, block.shape[dim] - width, None, axis=dim), axis, forward
        )
        high = lax.ppermute(lax.slice_in_dim(block, 0, width, axis=dim), axis, backward)
        block = jnp.concatenate([low, block, high], axis=dim)
    return block


def gelu_pair(value):
    coeff = 0.7978845608028654
    inner = coeff * (value + 0.044715 * value * value * value)
    tanh_val = jnp.tanh(inner)
    result = 0.5 * value * (1.0 + tanh_val)
    slope = 0.5 * (1.0 + tanh_val) + 0.5 * value * (1.0 - tanh_val * tanh_val) * coeff * (
        1.0 + 0.134145 * value * value
    )
    return (result, slope)


def depthwise(ext, kernel, nrows, ncols):
    total = jnp.zeros((nrows, ncols, kernel.shape[1]), jnp.float32)
    for tap_a in range(7):
        for tap_b in range(7):
            total = total + kernel[7 * tap_a + tap_b] * ext[
                tap_a : tap_a + nrows, tap_b : tap_b + ncols
            ].astype(jnp.float32)
    return total


def transposed(padded, kernel, nrows, ncols):
    total = jnp.zeros((nrows, ncols, kernel.shape[1]), jnp.float32)
    for tap_a in range(7):
        for tap_b in range(7):
            window = padded[6 - tap_a : 6 - tap_a + nrows, 6 - tap_b : 6 - tap_b + ncols].astype(
                jnp.float32
            )
            total = total + kernel[7 * tap_a + tap_b] * window
    return total


def local_block(conv_flat, field_flat, mask_col, cot_flat, norm_gain, proj_in, proj_out):
    mean = jnp.mean(conv_flat, axis=-1, keepdims=True)
    centered = conv_flat - mean
    var = jnp.mean(centered * centered, axis=-1, keepdims=True)
    rstd = lax.rsqrt(var + 1e-06)
    nhat = centered * rstd
    normed = (nhat * norm_gain).astype(jnp.bfloat16)
    pre = jnp.dot(normed, proj_in, preferred_element_type=jnp.float32)
    act, slope = gelu_pair(pre)
    act = act.astype(jnp.bfloat16)
    mixed = jnp.dot(act, proj_out, preferred_element_type=jnp.float32)
    result = (mask_col * (field_flat + mixed)).astype(jnp.bfloat16)
    back = cot_flat * mask_col
    dw_out = lax.dot_general(
        act, back, (((0,), (0,)), ((), ())), preferred_element_type=jnp.float32
    )
    grad_hidden = lax.dot_general(
        back, proj_out, (((1,), (1,)), ((), ())), preferred_element_type=jnp.float32
    )
    grad_pre = (grad_hidden * slope).astype(jnp.bfloat16)
    dw_in = lax.dot_general(
        normed, grad_pre, (((0,), (0,)), ((), ())), preferred_element_type=jnp.float32
    )
    grad_norm = lax.dot_general(
        grad_pre, proj_in, (((1,), (1,)), ((), ())), preferred_element_type=jnp.float32
    )
    dgain = jnp.sum(grad_norm * nhat, axis=0)
    scaled = grad_norm * norm_gain
    gconv = rstd * (
        scaled
        - jnp.mean(scaled, axis=-1, keepdims=True)
        - nhat * jnp.mean(scaled * nhat, axis=-1, keepdims=True)
    )
    return (result, gconv.astype(jnp.bfloat16), dw_in, dw_out, dgain)


def body(field_in, sea_mask, mirror, kernel, norm_gain, proj_in, proj_out, cotangent):
    nrows, ncols, width = field_in.shape
    n_lon = lax.axis_size("lon")
    n_lat = lax.axis_size("lat")
    total_cols = ncols * n_lon
    band = lax.axis_index("lat")
    is_top = band == n_lat - 1
    is_bottom = band == 0
    start = lax.axis_index("lon") * ncols
    maskf = sea_mask.astype(jnp.bfloat16)[:, :, None]
    masked = field_in * maskf
    ext = extended(masked, (("lat", 0), ("lon", 1)), 3)
    top_rows = lax.all_gather(masked[nrows - 3 :], "lon", axis=1, tiled=True)
    ext_cols = (start - 3 + jnp.arange(ncols + 6, dtype=jnp.int32)) % total_cols
    north = jnp.take(top_rows[::-1], jnp.take(mirror, ext_cols), axis=1)
    lower = jnp.where(is_bottom, jnp.zeros_like(ext[:3]), ext[:3])
    upper = jnp.where(is_top, north, ext[nrows + 3 :])
    ext = jnp.concatenate([lower, ext[3 : nrows + 3], upper], axis=0)
    conv = depthwise(ext, kernel, nrows, ncols)
    cells = nrows * ncols
    mask_col = maskf.reshape(cells, 1)
    block_out, gconv, dw_in, dw_out, dgain = local_block(
        conv.reshape(cells, width),
        field_in.reshape(cells, width),
        mask_col,
        cotangent.reshape(cells, width),
        norm_gain,
        proj_in,
        proj_out,
    )
    gconv = gconv.reshape(nrows, ncols, width)
    gconv_f = gconv.astype(jnp.float32)
    taps = []
    for tap_a in range(7):
        for tap_b in range(7):
            taps.append(
                jnp.sum(
                    gconv_f * ext[tap_a : tap_a + nrows, tap_b : tap_b + ncols].astype(jnp.float32),
                    axis=(0, 1),
                )
            )
    dkernel = jnp.stack(taps, axis=0)
    gext = extended(gconv, (("lat", 0), ("lon", 1)), 3)
    glower = jnp.where(is_bottom, jnp.zeros_like(gext[:3]), gext[:3])
    gupper = jnp.where(is_top, jnp.zeros_like(gext[:3]), gext[nrows + 3 :])
    spare = jnp.zeros((3, ncols + 6, width), jnp.bfloat16)
    gpad = jnp.concatenate([glower, gext[3 : nrows + 3], gupper, spare], axis=0)
    dfull = transposed(gpad, kernel, nrows + 3, ncols)
    own_mirror = jnp.take(mirror, start + jnp.arange(ncols, dtype=jnp.int32))
    fold_all = lax.all_gather(dfull[nrows:], "lon", axis=1, tiled=True)
    fold = jnp.take(fold_all[::-1], own_mirror, axis=1)
    fold = jnp.where(is_top, fold, jnp.zeros_like(fold))
    dmasked = dfull[:nrows] + jnp.concatenate(
        [jnp.zeros((nrows - 3, ncols, width), jnp.float32), fold], axis=0
    )
    back = (cotangent * maskf).astype(jnp.float32)
    grad_field = (back + maskf * dmasked).astype(jnp.bfloat16)
    sum_in, sum_out, sum_kernel, sum_gain = lax.psum(
        (dw_in, dw_out, dkernel, dgain), ("lat", "lon")
    )
    factor = 1.0 / jnp.sqrt(jnp.float32(nrows * n_lat * total_cols))
    return (
        block_out.reshape(nrows, ncols, width),
        grad_field,
        sum_in * factor,
        sum_out * factor,
        sum_kernel * factor,
        sum_gain * factor,
    )


def solution(mesh):
    in_specs = (
        P("lat", "lon", None),
        P("lat", "lon"),
        P(),
        P(),
        P(),
        P(),
        P(),
        P("lat", "lon", None),
    )
    out_specs = (P("lat", "lon", None), P("lat", "lon", None), P(), P(), P(), P())
    return jax.shard_map(body, mesh=mesh, in_specs=in_specs, out_specs=out_specs, check_vma=False)
```

profile of v0, /device:TPU:0, one launch (start us, length us, event | category | flops | bytes accessed | tf_op | source)
XLA Modules:
  0.0 347.3 jit_solution(4353511875321528051)
XLA Ops:
  20.4 3.1 collective-permute-start.3
  23.5 36.8 %all_gather.6 = bf16[3,64,300]{2,1,0:T(8,128)(2,1)S(1)} all-gather(bf16[3,8,300]{2,1,0:T(8,128)(2,1)S(1)} %copy.43), channel_id=1, replica_groups=mesh['lat'=4,'lon'=8] {'lon'}, dimensions={1}, use_global_device_ids=true | all-gather | bytes 129600 | tf_op jit(solution)/shard_map/all_gather | solution.py:101
  60.4 2.5 copy.52
  68.8 2.9 copy.49
  77.4 18.2 %fusion.173 = (f32[128,8]{0,1:T(8,128)S(1)}, f32[128,8,300]{2,0,1:T(8,128)S(1)}) fusion(bf16[3,14,300]{2,0,1:T(4,128)(2,1)S(1)} %get-tuple-element.142, bf16[128,14,300]{2,0,1:T(8,128)(2,1)S(1)} %slice.871, f32[300]{0:T(512)S(1)} %copy-done.109, f32[300]{0:T(512)S(1)} %copy-done.110, f32[300]{0:T(512)S(1)} %get-tuple-element.83, ...), kind=kLoop, calls=%fused_computation.453 | loop fusion | flops 84786176 | bytes 6720144 | tf_op jit(solution)/shard_map/reduce_sum | solution.py:54
  101.6 2.4 fusion.171
  104.1 4.7 %fusion.6 = bf16[1024,1200]{0,1:T(8,128)(2,1)S(1)} fusion(f32[1024,1200]{0,1:T(8,128)S(1)} %fusion.171, bf16[1200,300]{0,1:T(8,128)(2,1)S(1)} %copy-done.118, bf16[128,8,300]{2,1,0:T(8,128)(2,1)S(1)} %copy-done.15, bf16[1024]{0:T(1024)(128)(2,1)S(1)} %copy-done.114), kind=kOutput, calls=%fused_computation.101 | convolution fusion | flops 760934400 | bytes 8709248 | tf_op jit(solution)/shard_map/dot_general | solution.py:69
  113.1 4.7 %fusion.82 = (f32[300]{0:T(512)S(1)}, f32[300]{0:T(512)S(1)}, f32[300]{0:T(512)S(1)}, f32[300]{0:T(512)S(1)}, f32[300]{0:T(512)S(1)}, /*index=5*/f32[300]{0:T(512)S(1)}) fusion(bf16[134,11,300]{2,0,1:T(8,128)(2,1)} %copy-done.3, bf16[128,8,300]{2,1,0:T(8,128)(2,1)S(1)} %bitcast.38, bf16[134,11,300]{2,0,1:T(8,128)(2,1)} %copy-done.2), kind=kLoop, calls=%fused_computation.240 | loop fusion | flops 5835000 | bytes 4308000 | tf_op jit(solution)/shard_map/reduce_sum | solution.py:125
  117.8 2.6 fusion.100
  120.4 2.9 fusion.103
  129.9 2.6 fusion.102
  132.5 2.8 fusion.101
  137.6 3.2 fusion.161
  144.5 5.7 %fusion.108 = bf16[1024,300]{0,1:T(8,128)(2,1)} fusion(f32[1024,300]{0,1:T(8,128)} %copy.49, bf16[1200,300]{0,1:T(8,128)(2,1)} %param.14, f32[1024]{0:T(1024)S(1)} %copy-done.115, f32[1024,1200]{0,1:T(8,128)} %copy-done.9), kind=kOutput, calls=%fused_computation.274 | convolution fusion | flops 749260800 | bytes 7482496 | tf_op jit(solution)/shard_map/dot_general | solution.py:63
  150.5 38.7 %all-reduce.1 = (f32[49,300]{1,0:T(8,128)S(1)}, f32[300]{0:T(512)S(1)}) all-reduce(f32[49,300]{1,0:T(8,128)S(1)} %stack.199, f32[300]{0:T(512)S(1)} %get-tuple-element.24), channel_id=1, replica_groups=mesh['lat'=4,'lon'=8] {'lat','lon'}, use_global_device_ids=true, to_apply=%region_55.56 | all-reduce | flops 15000 | bytes 120000 | tf_op jit(solution)/shard_map/psum | solution.py:146
  192.3 2.5 collective-permute-start.7
  199.0 8.7 %collective-permute-done.6 = bf16[134,3,300]{2,0,1:T(8,128)(2,1)S(1)} collective-permute-done((bf16[134,3,300]{2,0,1:T(8,128)(2,1)}, bf16[134,3,300]{2,0,1:T(8,128)(2,1)S(1)}, u32[]{:S(2)}, u32[]{:S(2)}) %collective-permute-start.6) | collective-permute-done | bytes 241232 | tf_op jit(solution)/shard_map/ppermute | solution.py:13
  207.6 2.8 collective-permute-done.7
  213.0 18.6 %multiply_add_fusion.1 = f32[131,8,300]{2,0,1:T(8,128)S(1)} fusion(bf16[3,14,300]{2,0,1:T(4,128)(2,1)S(1)} %get-tuple-element.140, bf16[3,14,300]{2,0,1:T(4,128)(2,1)S(1)} %get-tuple-element.139, bf16[128,14,300]{2,0,1:T(8,128)(2,1)S(1)} %slice.960, bf16[134,14,300]{2,0,1:T(8,128)(2,1)S(1)} %get-tuple-element.144, ...), kind=kLoop, calls=%fused_computation.164 | loop fusion | flops 59107200 | bytes 24450000 | tf_op jit(solution)/shard_map/add | solution.py:49
  231.7 31.4 %all_gather.7 = f32[3,64,300]{2,1,0:T(8,128)S(1)} all-gather(f32[3,8,300]{2,1,0:T(8,128)S(1)} %copy.59), channel_id=1, replica_groups=mesh['lat'=4,'lon'=8] {'lon'}, dimensions={1}, use_global_device_ids=true | all-gather | bytes 259200 | tf_op jit(solution)/shard_map/all_gather | solution.py:138
  264.0 2.8 rev.7
  269.9 2.3 copy.63
  272.2 63.9 %all-reduce.5.cloned.1.call-done = (f32[300,1200]{1,0:T(8,128)}, f32[1200,300]{0,1:T(8,128)}) async-done(((f32[300,1200]{1,0:T(8,128)}, f32[1200,300]{0,1:T(8,128)}), (f32[300,1200]{1,0:T(8,128)}, f32[1200,300]{0,1:T(8,128)})) %all-reduce.5.cloned.1.call-update) | async-done | bytes 2880016 | tf_op jit(solution)/shard_map/psum | solution.py:146
  336.1 2.8 broadcast_multiply_fusion
  (384 shorter events, 60.8 us)
Async XLA Ops:
  7.2 94.5 %copy-start = (bf16[300,1200]{1,0:T(8,128)(2,1)S(1)}, bf16[300,1200]{1,0:T(8,128)(2,1)}, u32[]{:S(2)}) copy-start(bf16[300,1200]{1,0:T(8,128)(2,1)} %param.13) | copy-start | bytes 2160004
  7.2 328.9 %all-reduce.5.cloned.1.call-start = ((), (), s32[]{:S(2)}) async-start(), calls=%async_computation | async-start | bytes 6225920 | tf_op jit(solution)/shard_map/psum | solution.py:146
  8.6 67.3 %copy-start.19 = (bf16[128,8]{0,1:T(8,128)(2,1)}, bf16[128,8]{0,1:T(8,128)(2,1)S(1)}, u32[]{:S(2)}) copy-start(bf16[128,8]{0,1:T(8,128)(2,1)S(1)} %get-tuple-element.136) | copy-start | bytes 6148
  10.4 6.8 %collective-permute-start = (bf16[3,8,300]{2,0,1:T(4,128)(2,1)S(1)}, bf16[3,8,300]{2,0,1:T(4,128)(2,1)S(1)}, u32[]{:S(2)}, u32[]{:S(2)}) collective-permute-start(bf16[3,8,300]{2,0,1:T(4,128)(2,1)S(1)} %get-tuple-element.151), channel_id=1, source_target_pairs={{0,8},{8,16},{16,24},{24,0},{1,9},{9,17},{17,25},{25,1},{2,10},{10... | collective-permute-start | bytes 43208 | tf_op jit(solution)/shard_map/ppermute | solution.py:13
  10.9 6.3 %collective-permute-start.1 = (bf16[3,8,300]{2,0,1:T(4,128)(2,1)S(1)}, bf16[3,8,300]{2,0,1:T(4,128)(2,1)S(1)}, u32[]{:S(2)}, u32[]{:S(2)}) collective-permute-start(bf16[3,8,300]{2,0,1:T(4,128)(2,1)S(1)} %get-tuple-element.152), channel_id=1, source_target_pairs={{8,0},{16,8},{24,16},{0,24},{9,1},{17,9},{25,17},{1,25},{10,2},{18... | collective-permute-start | bytes 43208 | tf_op jit(solution)/shard_map/ppermute | solution.py:16
  14.3 61.6 %copy-start.24 = (f32[300]{0:T(512)}, f32[300]{0:T(512)S(1)}, u32[]{:S(2)}) copy-start(f32[300]{0:T(512)S(1)} %get-tuple-element.83) | copy-start | bytes 3604
  14.3 61.6 %copy-start.26 = (f32[300]{0:T(512)}, f32[300]{0:T(512)S(1)}, u32[]{:S(2)}) copy-start(f32[300]{0:T(512)S(1)} %get-tuple-element.84) | copy-start | bytes 3604
  14.3 61.6 %copy-start.28 = (f32[300]{0:T(512)}, f32[300]{0:T(512)S(1)}, u32[]{:S(2)}) copy-start(f32[300]{0:T(512)S(1)} %get-tuple-element.85) | copy-start | bytes 3604
  14.3 61.6 %copy-start.30 = (f32[300]{0:T(512)}, f32[300]{0:T(512)S(1)}, u32[]{:S(2)}) copy-start(f32[300]{0:T(512)S(1)} %get-tuple-element.86) | copy-start | bytes 3604
  14.3 61.6 %copy-start.32 = (f32[300]{0:T(512)}, f32[300]{0:T(512)S(1)}, u32[]{:S(2)}) copy-start(f32[300]{0:T(512)S(1)} %get-tuple-element.87) | copy-start | bytes 3604
  14.3 61.6 %copy-start.34 = (f32[300]{0:T(512)}, f32[300]{0:T(512)S(1)}, u32[]{:S(2)}) copy-start(f32[300]{0:T(512)S(1)} %get-tuple-element.88) | copy-start | bytes 3604
  14.3 61.6 %copy-start.36 = (f32[300]{0:T(512)}, f32[300]{0:T(512)S(1)}, u32[]{:S(2)}) copy-start(f32[300]{0:T(512)S(1)} %get-tuple-element.89) | copy-start | bytes 3604
  14.3 61.6 %copy-start.38 = (f32[300]{0:T(512)}, f32[300]{0:T(512)S(1)}, u32[]{:S(2)}) copy-start(f32[300]{0:T(512)S(1)} %get-tuple-element.90) | copy-start | bytes 3604
  14.3 61.6 %copy-start.40 = (f32[300]{0:T(512)}, f32[300]{0:T(512)S(1)}, u32[]{:S(2)}) copy-start(f32[300]{0:T(512)S(1)} %get-tuple-element.91) | copy-start | bytes 3604
  14.3 61.6 %copy-start.42 = (f32[300]{0:T(512)}, f32[300]{0:T(512)S(1)}, u32[]{:S(2)}) copy-start(f32[300]{0:T(512)S(1)} %get-tuple-element.92) | copy-start | bytes 3604
  14.4 61.6 %copy-start.44 = (f32[300]{0:T(512)}, f32[300]{0:T(512)S(1)}, u32[]{:S(2)}) copy-start(f32[300]{0:T(512)S(1)} %get-tuple-element.93) | copy-start | bytes 3604
  14.4 61.6 %copy-start.46 = (f32[300]{0:T(512)}, f32[300]{0:T(512)S(1)}, u32[]{:S(2)}) copy-start(f32[300]{0:T(512)S(1)} %get-tuple-element.94) | copy-start | bytes 3604
  14.4 61.6 %copy-start.48 = (f32[300]{0:T(512)}, f32[300]{0:T(512)S(1)}, u32[]{:S(2)}) copy-start(f32[300]{0:T(512)S(1)} %get-tuple-element.95) | copy-start | bytes 3604
  18.2 54.7 %collective-permute-start.2 = (bf16[134,3,300]{2,0,1:T(8,128)(2,1)}, bf16[134,3,300]{2,0,1:T(8,128)(2,1)S(1)}, u32[]{:S(2)}, u32[]{:S(2)}) collective-permute-start(bf16[134,3,300]{2,0,1:T(8,128)(2,1)} %get-tuple-element.149), channel_id=1, source_target_pairs={{0,1},{1,2},{2,3},{3,4},{4,5},{5,6},{6,7},{7,0},{8,9},{9,10},{10,1... | collective-permute-start | bytes 723608 | tf_op jit(solution)/shard_map/ppermute | solution.py:13
  20.4 52.5 %collective-permute-start.3 = (bf16[134,3,300]{2,0,1:T(8,128)(2,1)}, bf16[134,3,300]{2,0,1:T(8,128)(2,1)S(1)}, u32[]{:S(2)}, u32[]{:S(2)}) collective-permute-start(bf16[134,3,300]{2,0,1:T(8,128)(2,1)} %get-tuple-element.150), channel_id=1, source_target_pairs={{1,0},{2,1},{3,2},{4,3},{5,4},{6,5},{7,6},{0,7},{9,8},{10,9},{11,1... | collective-permute-start | bytes 723608 | tf_op jit(solution)/shard_map/ppermute | solution.py:16
  142.6 46.6 %collective-permute-start.4 = (bf16[3,8,300]{2,0,1:T(4,128)(2,1)S(1)}, bf16[3,8,300]{2,0,1:T(4,128)(2,1)S(1)}, u32[]{:S(2)}, u32[]{:S(2)}) collective-permute-start(bf16[3,8,300]{2,0,1:T(4,128)(2,1)S(1)} %copy.54), channel_id=1, source_target_pairs={{0,8},{8,16},{16,24},{24,0},{1,9},{9,17},{17,25},{25,1},{2,10},{10... | collective-permute-start | bytes 43208 | tf_op jit(solution)/shard_map/ppermute | solution.py:13
  142.7 46.5 %collective-permute-start.5 = (bf16[3,8,300]{2,0,1:T(4,128)(2,1)S(1)}, bf16[3,8,300]{2,0,1:T(4,128)(2,1)S(1)}, u32[]{:S(2)}, u32[]{:S(2)}) collective-permute-start(bf16[3,8,300]{2,0,1:T(4,128)(2,1)S(1)} %copy.57), channel_id=1, source_target_pairs={{8,0},{16,8},{24,16},{0,24},{9,1},{17,9},{25,17},{1,25},{10,2},{18... | collective-permute-start | bytes 43208 | tf_op jit(solution)/shard_map/ppermute | solution.py:16
  190.1 17.5 %collective-permute-start.6 = (bf16[134,3,300]{2,0,1:T(8,128)(2,1)}, bf16[134,3,300]{2,0,1:T(8,128)(2,1)S(1)}, u32[]{:S(2)}, u32[]{:S(2)}) collective-permute-start(bf16[134,3,300]{2,0,1:T(8,128)(2,1)} %get-tuple-element.145), channel_id=1, source_target_pairs={{0,1},{1,2},{2,3},{3,4},{4,5},{5,6},{6,7},{7,0},{8,9},{9,10},{10,1... | collective-permute-start | bytes 723608 | tf_op jit(solution)/shard_map/ppermute | solution.py:13
  192.3 18.1 %collective-permute-start.7 = (bf16[134,3,300]{2,0,1:T(8,128)(2,1)S(1)}, bf16[134,3,300]{2,0,1:T(8,128)(2,1)S(1)}, u32[]{:S(2)}, u32[]{:S(2)}) collective-permute-start(bf16[134,3,300]{2,0,1:T(8,128)(2,1)S(1)} %get-tuple-element.146), channel_id=1, source_target_pairs={{1,0},{2,1},{3,2},{4,3},{5,4},{6,5},{7,6},{0,7},{9,8},{10,9},{11,1... | collective-permute-start | bytes 723608 | tf_op jit(solution)/shard_map/ppermute | solution.py:16
  (108 other events, 1232.0 us)
Sparse Core Ops, SparseCore 0:
  198.5 137.5 all-reduce.4
where the time goes:
time: 351 us; the launch traced here: 347 us
  blocking collectives  107 us (30%)
  waiting for transfers between devices  75.4 us (21%)
  other arithmetic  74.8 us (21%)
  local copies, waits for them, and re-layouts  39.4 us (11%)
  matrix products  19.6 us (6%)
  between operations  16.6 us (5%)
  starting transfers between devices  14.4 us (4%)
    psum x1, waiting for transfers between devices, body(): lax.psum((dw_in, dw_out, dkernel, dgain), ('lat', 'lon'))  63.9 us
    psum x1, blocking collectives, body(): lax.psum((dw_in, dw_out, dkernel, dgain), ('lat', 'lon'))  38.7 us
    all_gather x1, blocking collectives, body(): top_rows = lax.all_gather(masked[nrows - 3:], 'lon', axis=1, tiled=True)  36.8 us
    all_gather x1, blocking collectives, body(): fold_all = lax.all_gather(dfull[nrows:], 'lon', axis=1, tiled=True)  31.4 us
    reduce_sum x8, other arithmetic, body(): jnp.sum(gconv_f * ext[tap_a:tap_a + nrows, tap_b:tap_b + ncols].astype(jn...  22.1 us
    add x1, other arithmetic, transposed(): total = total + kernel[7 * tap_a + tap_b] * window  18.6 us
    reduce_sum x1, other arithmetic, local_block(): mean = jnp.mean(conv_flat, axis=-1, keepdims=True)  18.2 us
    unnamed x251, local copies, waits for them, and re-layouts  13.5 us
  transfers between devices with their start and end apart: 9, of which 3 were waited for; matrix products, arithmetic and copies ran while one was open for 16% of the time, Pallas kernels for 0%

commit v1 on v0

--- a/solution.py
+++ b/solution.py
@@ -98,7 +98,20 @@
     maskf = sea_mask.astype(jnp.bfloat16)[:, :, None]
     masked = field_in * maskf
     ext = extended(masked, (("lat", 0), ("lon", 1)), 3)
-    top_rows = lax.all_gather(masked[nrows - 3 :], "lon", axis=1, tiled=True)
+    x = masked[nrows - 3 :]
+    ways, here, lap = (lax.axis_size("lon"), lax.axis_index("lon"), x.shape[1])
+    lengths = [n * ways if d == 1 else n for d, n in enumerate(x.shape)]
+    full = lax.dynamic_update_slice_in_dim(jnp.zeros(lengths, x.dtype), x, here * lap, axis=1)
+    going_up = going_down = x
+    for far in range(1, ways // 2 + 1):
+        going_up = lax.ppermute(going_up, "lon", [(d, (d + 1) % ways) for d in range(ways)])
+        full = lax.dynamic_update_slice_in_dim(full, going_up, (here - far) % ways * lap, axis=1)
+        if 2 * far < ways:
+            going_down = lax.ppermute(going_down, "lon", [(d, (d - 1) % ways) for d in range(ways)])
+            full = lax.dynamic_update_slice_in_dim(
+                full, going_down, (here + far) % ways * lap, axis=1
+            )
+    top_rows = full
     ext_cols = (start - 3 + jnp.arange(ncols + 6, dtype=jnp.int32)) % total_cols
     north = jnp.take(top_rows[::-1], jnp.take(mirror, ext_cols), axis=1)
     lower = jnp.where(is_bottom, jnp.zeros_like(ext[:3]), ext[:3])

time: 351 us -> 338 us (0.963)
  blocking collectives: 107 us -> 69 us
  starting transfers between devices: 14.4 us -> 29.2 us
  waiting for transfers between devices: 75.4 us -> 87.8 us
    all_gather x1 -> x0, blocking collectives: 36.8 us -> none  [body(): top_rows = lax.all_gather(masked[nrows - 3:], 'lon', axis=1, tiled=True)]
    ppermute x0 -> x7, starting transfers between devices: none -> 15.9 us  [the longest x3 10 us: body(): lax.ppermute(going_down, 'lon', [(d, (d - 1) % ways) for d in range(ways)])]
    ppermute x0 -> x7, waiting for transfers between devices: none -> 13 us  [the longest x4 13 us: body(): lax.ppermute(going_up, 'lon', [(d, (d + 1) % ways) for d in range(ways)])]
    unnamed x251 -> x231, local copies, waits for them, and re-layouts: 13.5 us -> 9.99 us
  transfers between devices with their start and end apart: 9 -> 16, of which waited for: 3 -> 6; matrix products, arithmetic and copies ran while one was open for 16% -> 17% of each run, Pallas kernels for 0% -> 0%
where the time goes in v1:
time: 338 us; the launch traced here: 333 us
  waiting for transfers between devices  87.8 us (26%)
  other arithmetic  72.8 us (22%)
  blocking collectives  69 us (20%)
  local copies, waits for them, and re-layouts  38.5 us (11%)
  starting transfers between devices  29.2 us (9%)
  matrix products  19.4 us (6%)
  between operations  16.6 us (5%)
    psum x1, waiting for transfers between devices, body(): lax.psum((dw_in, dw_out, dkernel, dgain), ('lat', 'lon'))  62.5 us
    psum x1, blocking collectives, body(): lax.psum((dw_in, dw_out, dkernel, dgain), ('lat', 'lon'))  37.9 us
    all_gather x1, blocking collectives, body(): fold_all = lax.all_gather(dfull[nrows:], 'lon', axis=1, tiled=True)  31.1 us
    reduce_sum x8, other arithmetic, body(): jnp.sum(gconv_f * ext[tap_a:tap_a + nrows, tap_b:tap_b + ncols].astype(jn...  19.5 us
    add x1, other arithmetic, transposed(): total = total + kernel[7 * tap_a + tap_b] * window  18.5 us
    reduce_sum x1, other arithmetic, local_block(): mean = jnp.mean(conv_flat, axis=-1, keepdims=True)  17.4 us
    ppermute x4, waiting for transfers between devices, body(): lax.ppermute(going_up, 'lon', [(d, (d + 1) % ways) for d in range(ways)])  13 us
    ppermute x4, starting transfers between devices, extended(): lax.ppermute(lax.slice_in_dim(block, 0, width, axis=dim), axis, backward)  11 us
  transfers between devices with their start and end apart: 16, of which 6 were waited for; matrix products, arithmetic and copies ran while one was open for 17% of the time, Pallas kernels for 0%

profile of v1, /device:TPU:0, one launch (start us, length us, event | category | flops | bytes accessed | tf_op | source)
XLA Modules:
  0.0 333.3 jit_solution(10779076563179092464)
XLA Ops:
  11.1 2.9 collective-permute-start.4
  14.0 3.0 collective-permute-start.5
  27.4 2.7 copy.41
  30.9 2.9 copy.47
  34.1 4.7 %collective-permute-start.3 = (bf16[134,3,300]{2,0,1:T(8,128)(2,1)S(1)}, bf16[134,3,300]{2,0,1:T(8,128)(2,1)S(1)}, u32[]{:S(2)}, u32[]{:S(2)}) collective-permute-start(bf16[134,3,300]{2,0,1:T(8,128)(2,1)S(1)} %get-tuple-element.150), channel_id=1, source_target_pairs={{1,0},{2,1},{3,2},{4,3},{5,4},{6,5},{7,6},{0,7},{9,8},{10,9},{11,1... | collective-permute-start | bytes 723608 | tf_op jit(solution)/shard_map/ppermute | solution.py:16
  38.8 4.7 %collective-permute-start.7 = (bf16[3,8,300]{2,0,1:T(4,128)(2,1)S(1)}, bf16[3,8,300]{2,0,1:T(4,128)(2,1)S(1)}, u32[]{:S(2)}, u32[]{:S(2)}) collective-permute-start(bf16[3,8,300]{2,0,1:T(4,128)(2,1)S(1)} %collective-permute-done.5), channel_id=1, source_target_pairs={{0,7},{1,0},{2,1},{3,2},{4,3},{5,4},{6,5},{7,6},{8,15},{9,8},{10,9... | collective-permute-start | bytes 43208 | tf_op jit(solution)/shard_map/ppermute | solution.py:110
  44.3 4.7 %collective-permute-done.6 = bf16[3,8,300]{2,0,1:T(4,128)(2,1)S(1)} collective-permute-done((bf16[3,8,300]{2,0,1:T(4,128)(2,1)}, bf16[3,8,300]{2,0,1:T(4,128)(2,1)S(1)}, u32[]{:S(2)}, u32[]{:S(2)}) %collective-permute-start.6) | collective-permute-done | bytes 14432 | tf_op jit(solution)/shard_map/ppermute | solution.py:107
  56.1 6.4 %collective-permute-done.10 = bf16[3,8,300]{2,0,1:T(4,128)(2,1)S(1)} collective-permute-done((bf16[3,8,300]{2,0,1:T(4,128)(2,1)S(1)}, bf16[3,8,300]{2,0,1:T(4,128)(2,1)S(1)}, u32[]{:S(2)}, u32[]{:S(2)}) %collective-permute-start.10) | collective-permute-done | bytes 14432 | tf_op jit(solution)/shard_map/ppermute | solution.py:107
  68.6 17.4 %fusion.173 = (f32[128,8]{0,1:T(8,128)S(1)}, f32[128,8,300]{2,0,1:T(8,128)S(1)}) fusion(bf16[3,14,300]{2,0,1:T(4,128)(2,1)S(1)} %get-tuple-element.142, bf16[128,14,300]{2,0,1:T(8,128)(2,1)S(1)} %slice.871, f32[300]{0:T(512)} %get-tuple-element.129, f32[300]{0:T(512)} %get-tuple-element.130, f32[300]{0:T(512)S(1)} %copy-done.30, f32[300]{0:T(512)S(1)} %copy-done.32, ...), kind=kLoop, calls=%fused_computation.461 | loop fusion | flops 84786176 | bytes 6720144 | tf_op jit(solution)/shard_map/reduce_sum | solution.py:54
  94.5 4.6 %fusion.6 = bf16[1024,1200]{0,1:T(8,128)(2,1)S(1)} fusion(f32[1024,1200]{0,1:T(8,128)S(1)} %fusion.171, bf16[1200,300]{0,1:T(8,128)(2,1)S(1)} %copy-done.108, bf16[128,8,300]{2,1,0:T(8,128)(2,1)S(1)} %copy-done.16, bf16[1024]{0:T(1024)(128)(2,1)S(1)} %copy-done.105), kind=kOutput, calls=%fused_computation.101 | convolution fusion | flops 760934400 | bytes 8709248 | tf_op jit(solution)/shard_map/dot_general | solution.py:69
  103.3 4.1 %fusion.103 = (f32[300]{0:T(512)S(1)}, f32[300]{0:T(512)S(1)}, f32[300]{0:T(512)S(1)}, f32[300]{0:T(512)S(1)}, f32[300]{0:T(512)S(1)}, /*index=5*/f32[300]{0:T(512)S(1)}, f32[300]{0:T(512)S(1)}) fusion(bf16[3,14,300]{2,0,1:T(4,128)(2,1)S(1)} %get-tuple-element.142, bf16[128,14,300]{2,0,1:T(8,128)(2,1)S(1)} %slice.871, bf16[128,8,300]{2,1,0:T(8,128)(2,1)S(1)} %bitcast.38, ...), kind=kLoop, calls=%fused_computation.261 | loop fusion | flops 13207500 | bytes 2339648 | tf_op jit(solution)/shard_map/reduce_sum | solution.py:138
  108.6 2.6 fusion.100
  117.7 2.6 fusion.102
  120.3 2.6 fusion.101
  125.2 3.2 fusion.161
  132.4 5.7 %fusion.108 = bf16[1024,300]{0,1:T(8,128)(2,1)} fusion(f32[1024,300]{0,1:T(8,128)} %copy.47, bf16[1200,300]{0,1:T(8,128)(2,1)} %param.14, f32[1024]{0:T(1024)S(1)} %copy-done.106, f32[1024,1200]{0,1:T(8,128)} %copy-done.10), kind=kOutput, calls=%fused_computation.274 | convolution fusion | flops 749260800 | bytes 7482496 | tf_op jit(solution)/shard_map/dot_general | solution.py:63
  138.3 37.9 %all-reduce.1 = (f32[49,300]{1,0:T(8,128)S(1)}, f32[300]{0:T(512)S(1)}) all-reduce(f32[49,300]{1,0:T(8,128)S(1)} %stack.199, f32[300]{0:T(512)S(1)} %get-tuple-element.24), channel_id=1, replica_groups=mesh['lat'=4,'lon'=8] {'lat','lon'}, use_global_device_ids=true, to_apply=%region_55.56 | all-reduce | flops 15000 | bytes 120000 | tf_op jit(solution)/shard_map/psum | solution.py:159
  186.0 7.4 %collective-permute-done.13 = bf16[134,3,300]{2,0,1:T(8,128)(2,1)S(1)} collective-permute-done((bf16[134,3,300]{2,0,1:T(8,128)(2,1)}, bf16[134,3,300]{2,0,1:T(8,128)(2,1)S(1)}, u32[]{:S(2)}, u32[]{:S(2)}) %collective-permute-start.13) | collective-permute-done | bytes 241232 | tf_op jit(solution)/shard_map/ppermute | solution.py:13
  193.3 4.9 %collective-permute-done.14 = bf16[134,3,300]{2,0,1:T(8,128)(2,1)S(1)} collective-permute-done((bf16[134,3,300]{2,0,1:T(8,128)(2,1)S(1)}, bf16[134,3,300]{2,0,1:T(8,128)(2,1)S(1)}, u32[]{:S(2)}, u32[]{:S(2)}) %collective-permute-start.14) | collective-permute-done | bytes 241232 | tf_op jit(solution)/shard_map/ppermute | solution.py:16
  200.7 18.5 %multiply_add_fusion.1 = f32[131,8,300]{2,0,1:T(8,128)S(1)} fusion(bf16[3,14,300]{2,0,1:T(4,128)(2,1)S(1)} %get-tuple-element.140, bf16[3,14,300]{2,0,1:T(4,128)(2,1)S(1)} %get-tuple-element.139, bf16[128,14,300]{2,0,1:T(8,128)(2,1)S(1)} %slice.960, bf16[134,14,300]{2,0,1:T(8,128)(2,1)S(1)} %get-tuple-element.144, ...), kind=kLoop, calls=%fused_computation.164 | loop fusion | flops 59107200 | bytes 24450000 | tf_op jit(solution)/shard_map/add | solution.py:49
  219.3 31.1 %all_gather.3 = f32[3,64,300]{2,1,0:T(8,128)S(1)} all-gather(f32[3,8,300]{2,1,0:T(8,128)S(1)} %copy.57), channel_id=1, replica_groups=mesh['lat'=4,'lon'=8] {'lon'}, dimensions={1}, use_global_device_ids=true | all-gather | bytes 259200 | tf_op jit(solution)/shard_map/all_gather | solution.py:151
  251.4 2.8 rev.7
  259.6 62.5 %all-reduce.5.cloned.1.call-done = (f32[300,1200]{1,0:T(8,128)}, f32[1200,300]{0,1:T(8,128)}) async-done(((f32[300,1200]{1,0:T(8,128)}, f32[1200,300]{0,1:T(8,128)}), (f32[300,1200]{1,0:T(8,128)}, f32[1200,300]{0,1:T(8,128)})) %all-reduce.5.cloned.1.call-update) | async-done | bytes 2880016 | tf_op jit(solution)/shard_map/psum | solution.py:159
  322.1 2.8 broadcast_multiply_fusion
  (383 shorter events, 73.9 us)
Async XLA Ops:
  7.2 84.9 %copy-start = (bf16[300,1200]{1,0:T(8,128)(2,1)S(1)}, bf16[300,1200]{1,0:T(8,128)(2,1)}, u32[]{:S(2)}) copy-start(bf16[300,1200]{1,0:T(8,128)(2,1)} %param.13) | copy-start | bytes 2160004
  7.2 314.9 %all-reduce.5.cloned.1.call-start = ((), (), s32[]{:S(2)}) async-start(), calls=%async_computation | async-start | bytes 6225920 | tf_op jit(solution)/shard_map/psum | solution.py:159
  10.1 23.7 %copy-start.8 = (bf16[128,8,300]{2,0,1:T(8,128)(2,1)}, bf16[128,8,300]{2,0,1:T(8,128)(2,1)S(1)}, u32[]{:S(2)}) copy-start(bf16[128,8,300]{2,0,1:T(8,128)(2,1)S(1)} %copy.42) | copy-start | bytes 1843204
  11.1 27.8 %collective-permute-start.4 = (bf16[3,8,300]{2,0,1:T(4,128)(2,1)}, bf16[3,8,300]{2,0,1:T(4,128)(2,1)}, u32[]{:S(2)}, u32[]{:S(2)}) collective-permute-start(bf16[3,8,300]{2,0,1:T(4,128)(2,1)} %get-tuple-element.153), channel_id=1, source_target_pairs={{0,1},{1,2},{2,3},{3,4},{4,5},{5,6},{6,7},{7,0},{8,9},{9,10},{10,1... | collective-permute-start | bytes 43208 | tf_op jit(solution)/shard_map/ppermute | solution.py:107
  14.0 24.8 %collective-permute-start.5 = (bf16[3,8,300]{2,0,1:T(4,128)(2,1)}, bf16[3,8,300]{2,0,1:T(4,128)(2,1)S(1)}, u32[]{:S(2)}, u32[]{:S(2)}) collective-permute-start(bf16[3,8,300]{2,0,1:T(4,128)(2,1)} %get-tuple-element.153), channel_id=1, source_target_pairs={{0,7},{1,0},{2,1},{3,2},{4,3},{5,4},{6,5},{7,6},{8,15},{9,8},{10,9... | collective-permute-start | bytes 43208 | tf_op jit(solution)/shard_map/ppermute | solution.py:110
  17.0 16.8 %collective-permute-start = (bf16[3,8,300]{2,0,1:T(4,128)(2,1)}, bf16[3,8,300]{2,0,1:T(4,128)(2,1)S(1)}, u32[]{:S(2)}, u32[]{:S(2)}) collective-permute-start(bf16[3,8,300]{2,0,1:T(4,128)(2,1)} %get-tuple-element.153), channel_id=1, source_target_pairs={{0,8},{8,16},{16,24},{24,0},{1,9},{9,17},{17,25},{25,1},{2,10},{10... | collective-permute-start | bytes 43208 | tf_op jit(solution)/shard_map/ppermute | solution.py:13
  17.0 16.8 %collective-permute-start.1 = (bf16[3,8,300]{2,0,1:T(4,128)(2,1)S(1)}, bf16[3,8,300]{2,0,1:T(4,128)(2,1)S(1)}, u32[]{:S(2)}, u32[]{:S(2)}) collective-permute-start(bf16[3,8,300]{2,0,1:T(4,128)(2,1)S(1)} %get-tuple-element.152), channel_id=1, source_target_pairs={{8,0},{16,8},{24,16},{0,24},{9,1},{17,9},{25,17},{1,25},{10,2},{18... | collective-permute-start | bytes 43208 | tf_op jit(solution)/shard_map/ppermute | solution.py:16
  33.8 30.0 %copy-start.18 = (bf16[3,8,300]{2,0,1:T(4,128)(2,1)}, bf16[3,8,300]{2,0,1:T(4,128)(2,1)S(1)}, u32[]{:S(2)}) copy-start(bf16[3,8,300]{2,0,1:T(4,128)(2,1)S(1)} %collective-permute-done) | copy-start | bytes 43204
  33.8 30.0 %copy-start.20 = (bf16[3,8,300]{2,0,1:T(4,128)(2,1)}, bf16[3,8,300]{2,0,1:T(4,128)(2,1)S(1)}, u32[]{:S(2)}) copy-start(bf16[3,8,300]{2,0,1:T(4,128)(2,1)S(1)} %collective-permute-done.1) | copy-start | bytes 43204
  34.0 29.8 %collective-permute-start.2 = (bf16[134,3,300]{2,0,1:T(8,128)(2,1)S(1)}, bf16[134,3,300]{2,0,1:T(8,128)(2,1)S(1)}, u32[]{:S(2)}, u32[]{:S(2)}) collective-permute-start(bf16[134,3,300]{2,0,1:T(8,128)(2,1)S(1)} %get-tuple-element.149), channel_id=1, source_target_pairs={{0,1},{1,2},{2,3},{3,4},{4,5},{5,6},{6,7},{7,0},{8,9},{9,10},{10,1... | collective-permute-start | bytes 723608 | tf_op jit(solution)/shard_map/ppermute | solution.py:13
  34.1 29.7 %collective-permute-start.3 = (bf16[134,3,300]{2,0,1:T(8,128)(2,1)S(1)}, bf16[134,3,300]{2,0,1:T(8,128)(2,1)S(1)}, u32[]{:S(2)}, u32[]{:S(2)}) collective-permute-start(bf16[134,3,300]{2,0,1:T(8,128)(2,1)S(1)} %get-tuple-element.150), channel_id=1, source_target_pairs={{1,0},{2,1},{3,2},{4,3},{5,4},{6,5},{7,6},{0,7},{9,8},{10,9},{11,1... | collective-permute-start | bytes 723608 | tf_op jit(solution)/shard_map/ppermute | solution.py:16
  38.8 10.2 %collective-permute-start.6 = (bf16[3,8,300]{2,0,1:T(4,128)(2,1)}, bf16[3,8,300]{2,0,1:T(4,128)(2,1)S(1)}, u32[]{:S(2)}, u32[]{:S(2)}) collective-permute-start(bf16[3,8,300]{2,0,1:T(4,128)(2,1)} %collective-permute-done.4), channel_id=1, source_target_pairs={{0,1},{1,2},{2,3},{3,4},{4,5},{5,6},{6,7},{7,0},{8,9},{9,10},{10,1... | collective-permute-start | bytes 43208 | tf_op jit(solution)/shard_map/ppermute | solution.py:107
  38.8 12.7 %collective-permute-start.7 = (bf16[3,8,300]{2,0,1:T(4,128)(2,1)S(1)}, bf16[3,8,300]{2,0,1:T(4,128)(2,1)S(1)}, u32[]{:S(2)}, u32[]{:S(2)}) collective-permute-start(bf16[3,8,300]{2,0,1:T(4,128)(2,1)S(1)} %collective-permute-done.5), channel_id=1, source_target_pairs={{0,7},{1,0},{2,1},{3,2},{4,3},{5,4},{6,5},{7,6},{8,15},{9,8},{10,9... | collective-permute-start | bytes 43208 | tf_op jit(solution)/shard_map/ppermute | solution.py:110
  49.0 6.6 %collective-permute-start.8 = (bf16[3,8,300]{2,0,1:T(4,128)(2,1)S(1)}, bf16[3,8,300]{2,0,1:T(4,128)(2,1)S(1)}, u32[]{:S(2)}, u32[]{:S(2)}) collective-permute-start(bf16[3,8,300]{2,0,1:T(4,128)(2,1)S(1)} %collective-permute-done.6), channel_id=1, source_target_pairs={{0,1},{1,2},{2,3},{3,4},{4,5},{5,6},{6,7},{7,0},{8,9},{9,10},{10,1... | collective-permute-start | bytes 43208 | tf_op jit(solution)/shard_map/ppermute | solution.py:107
  51.5 4.6 %collective-permute-start.9 = (bf16[3,8,300]{2,0,1:T(4,128)(2,1)S(1)}, bf16[3,8,300]{2,0,1:T(4,128)(2,1)S(1)}, u32[]{:S(2)}, u32[]{:S(2)}) collective-permute-start(bf16[3,8,300]{2,0,1:T(4,128)(2,1)S(1)} %collective-permute-done.7), channel_id=1, source_target_pairs={{0,7},{1,0},{2,1},{3,2},{4,3},{5,4},{6,5},{7,6},{8,15},{9,8},{10,9... | collective-permute-start | bytes 43208 | tf_op jit(solution)/shard_map/ppermute | solution.py:110
  55.6 7.0 %collective-permute-start.10 = (bf16[3,8,300]{2,0,1:T(4,128)(2,1)S(1)}, bf16[3,8,300]{2,0,1:T(4,128)(2,1)S(1)}, u32[]{:S(2)}, u32[]{:S(2)}) collective-permute-start(bf16[3,8,300]{2,0,1:T(4,128)(2,1)S(1)} %collective-permute-done.8), channel_id=1, source_target_pairs={{0,1},{1,2},{2,3},{3,4},{4,5},{5,6},{6,7},{7,0},{8,9},{9,10},{10,1... | collective-permute-start | bytes 43208 | tf_op jit(solution)/shard_map/ppermute | solution.py:107
  66.2 19.8 %copy-start.2 = (bf16[134,11,300]{2,0,1:T(8,128)(2,1)}, bf16[134,11,300]{2,0,1:T(8,128)(2,1)S(1)}, u32[]{:S(2)}) copy-start(bf16[134,11,300]{2,0,1:T(8,128)(2,1)S(1)} %get-tuple-element.147) | copy-start | bytes 2653204
  130.2 46.0 %collective-permute-start.11 = (bf16[3,8,300]{2,0,1:T(4,128)(2,1)S(1)}, bf16[3,8,300]{2,0,1:T(4,128)(2,1)S(1)}, u32[]{:S(2)}, u32[]{:S(2)}) collective-permute-start(bf16[3,8,300]{2,0,1:T(4,128)(2,1)S(1)} %copy.52), channel_id=1, source_target_pairs={{0,8},{8,16},{16,24},{24,0},{1,9},{9,17},{17,25},{25,1},{2,10},{10... | collective-permute-start | bytes 43208 | tf_op jit(solution)/shard_map/ppermute | solution.py:13
  130.4 45.9 %collective-permute-start.12 = (bf16[3,8,300]{2,0,1:T(4,128)(2,1)S(1)}, bf16[3,8,300]{2,0,1:T(4,128)(2,1)S(1)}, u32[]{:S(2)}, u32[]{:S(2)}) collective-permute-start(bf16[3,8,300]{2,0,1:T(4,128)(2,1)S(1)} %copy.55), channel_id=1, source_target_pairs={{8,0},{16,8},{24,16},{0,24},{9,1},{17,9},{25,17},{1,25},{10,2},{18... | collective-permute-start | bytes 43208 | tf_op jit(solution)/shard_map/ppermute | solution.py:16
  177.1 16.2 %collective-permute-start.13 = (bf16[134,3,300]{2,0,1:T(8,128)(2,1)}, bf16[134,3,300]{2,0,1:T(8,128)(2,1)S(1)}, u32[]{:S(2)}, u32[]{:S(2)}) collective-permute-start(bf16[134,3,300]{2,0,1:T(8,128)(2,1)} %get-tuple-element.145), channel_id=1, source_target_pairs={{0,1},{1,2},{2,3},{3,4},{4,5},{5,6},{6,7},{7,0},{8,9},{9,10},{10,1... | collective-permute-start | bytes 723608 | tf_op jit(solution)/shard_map/ppermute | solution.py:13
  179.3 18.9 %collective-permute-start.14 = (bf16[134,3,300]{2,0,1:T(8,128)(2,1)S(1)}, bf16[134,3,300]{2,0,1:T(8,128)(2,1)S(1)}, u32[]{:S(2)}, u32[]{:S(2)}) collective-permute-start(bf16[134,3,300]{2,0,1:T(8,128)(2,1)S(1)} %get-tuple-element.146), channel_id=1, source_target_pairs={{1,0},{2,1},{3,2},{4,3},{5,4},{6,5},{7,6},{0,7},{9,8},{10,9},{11,1... | collective-permute-start | bytes 723608 | tf_op jit(solution)/shard_map/ppermute | solution.py:16
  219.3 36.7 %copy-start.11 = (bf16[128,8,300]{2,0,1:T(8,128)(2,1)S(1)}, bf16[128,8,300]{2,0,1:T(8,128)(2,1)}, u32[]{:S(2)}) copy-start(bf16[128,8,300]{2,0,1:T(8,128)(2,1)} %copy.49) | copy-start | bytes 1843204
  219.3 36.6 %copy-start.107 = (pred[8]{0:T(512)(128)(4,1)S(1)}, pred[8]{0:T(512)(128)(4,1)}, u32[]{:S(2)}) copy-start(pred[8]{0:T(512)(128)(4,1)} %compare_and_fusion) | copy-start | bytes 28
  219.3 36.7 %copy-start.103 = (f32[128,8]{0,1:T(8,128)S(1)}, f32[128,8]{0,1:T(8,128)}, u32[]{:S(2)}) copy-start(f32[128,8]{0,1:T(8,128)} %get-tuple-element.135) | copy-start | bytes 12292
  (105 other events, 271.8 us)
Sparse Core Ops, SparseCore 0:
  185.5 136.6 all-reduce.4
